TPU v7x, 32 devices: a whole 2x2x4 slice. The times are simulated.
32 devices in a mesh: groups: 2 (over y), ctx: 4 (over z), tm: 2 (over x), tp: 2 (over core).
Axes of the slice: x: 2, y: 2, z: 4, core: 2. Of those that a mesh axis runs over, the one named last changes fastest.
Arguments:
- tokens: bfloat16 [256, 8, 1024], P(('groups', 'tm'), 'ctx'), parts along dimension 0, may hold values from -6 to 6
- norm_gain: float32 [1024], replicated, may hold values from 0.1 to 1.9
- block_mask: int32 [4, 4, 4], P(('groups', 'tm'), 'ctx'), parts along dimension 0, may hold values from 0 to 1, as said below
- w_query: bfloat16 [1024, 1024], P('tm', 'tp'), may hold values from -1.25 to 1.25
- w_key: bfloat16 [1024, 1024], P('tm', 'tp'), may hold values from -1.25 to 1.25
- w_value: bfloat16 [1024, 1024], P('tm', 'tp'), may hold values from -0.1875 to 0.1875
- w_out: bfloat16 [1024, 1024], P('tp', 'tm'), may hold values from -0.1875 to 0.1875
- w_up: bfloat16 [1024, 2048], P('tm', 'tp'), may hold values from -0.1875 to 0.1875
- w_down: bfloat16 [2048, 1024], P('tp', 'tm'), may hold values from -0.125 to 0.125
- conv_weight: float32 [5, 1024], P(None, 'tp'), may hold values from -2.5 to 2.5
Outputs:
- denoised: bfloat16 [256, 8, 1024], P(('groups', 'tm'), 'ctx', 'tp'), parts along dimension 0
There are 2 independent parts, one for each index of `groups`. A program takes and returns all parts, laid end to end along the dimension named above; an argument that names none is the same for every part. Nothing has to cross between parts.
Inputs may be any that keep to these rules, and one draw needn't show every extreme that they name: block_mask[w, i, i] is 1 for every window w and block i.
All inputs are finite; a program needn't handle non-finite values.
Results may differ from a plain program's by a relative error of at most 0.0076.
Values may be sent and summed in bfloat16 or wider, within the bound.
A program may use at most 64 MiB of HBM per device.

v0:
```python
import jax
import jax.numpy as jnp
from jax import lax
from jax.sharding import PartitionSpec as P

HEAD_DIM = 64
KERNEL = 5


def from_behind(value, axis, steps):
    count = lax.axis_size(axis)
    first, last = (max(0, -steps), min(count, count - steps))
    return lax.ppermute(value, axis, [(source, source + steps) for source in range(first, last)])


def rms_norm(tokens, norm_gain):
    values = tokens.astype(jnp.float32)
    square = jnp.mean(values * values, axis=-1, keepdims=True)
    return (values * lax.rsqrt(square + 1e-05) * norm_gain).astype(jnp.bfloat16)


def on_device(
    tokens, norm_gain, block_mask, w_query, w_key, w_value, w_out, w_up, w_down, conv_weight
):
    frames_here, dancers_here, width = tokens.shape
    rows_here = frames_here * dancers_here
    normed_grid = rms_norm(tokens, norm_gain)
    normed = normed_grid.reshape(rows_here, width)
    pieces = (
        lax.all_gather(w_query, "tm", axis=0, tiled=True),
        lax.all_gather(w_key, "tm", axis=0, tiled=True),
        lax.all_gather(w_value, "tm", axis=0, tiled=True),
        lax.all_gather(w_up, "tm", axis=0, tiled=True),
    )
    query_sum, key_sum, value_sum, hidden = tuple(
        (jnp.dot(normed, piece_one, preferred_element_type=jnp.float32) for piece_one in pieces)
    )
    local_heads = query_sum.shape[1] // HEAD_DIM
    queries = query_sum.astype(jnp.bfloat16).reshape(rows_here, local_heads, HEAD_DIM)
    key_grid = key_sum.astype(jnp.bfloat16).reshape(
        frames_here, dancers_here, local_heads * HEAD_DIM
    )
    value_grid = value_sum.astype(jnp.bfloat16).reshape(
        frames_here, dancers_here, local_heads * HEAD_DIM
    )
    mask_row = block_mask[0, 0].astype(jnp.float32)
    cycle_blocks = mask_row.shape[0]
    key_piece = lax.all_gather(key_grid, "ctx", axis=1, tiled=True)
    value_piece = lax.all_gather(value_grid, "ctx", axis=1, tiled=True)
    count = key_piece.shape[1]
    block_ids = jnp.arange(count) // dancers_here
    picker = (block_ids[:, None] == jnp.arange(cycle_blocks)[None, :]).astype(jnp.float32)
    allowed_dancers = jnp.dot(picker, mask_row)
    peak_old = jnp.full((local_heads, rows_here), -1e30, jnp.float32)
    key_rows = key_piece.reshape(frames_here * count, local_heads, HEAD_DIM)
    value_rows = value_piece.reshape(frames_here * count, local_heads, HEAD_DIM)
    allowed = jnp.tile(allowed_dancers, frames_here)
    scores = (
        jnp.einsum("qhd,khd->hqk", queries, key_rows, preferred_element_type=jnp.float32) * 0.125
    )
    scores = jnp.where(allowed[None, None, :] > 0, scores, -1e30)
    peak_new = jnp.maximum(peak_old, jnp.max(scores, axis=-1))
    expo = jnp.exp(scores - peak_new[:, :, None]) * allowed[None, None, :]
    total_new = jnp.sum(expo, axis=-1)
    probs = expo.astype(jnp.bfloat16)
    mixed_new = jnp.einsum("hqk,khd->hqd", probs, value_rows, preferred_element_type=jnp.float32)
    attended = (
        (mixed_new / total_new[:, :, None])
        .transpose(1, 0, 2)
        .reshape(rows_here, local_heads * HEAD_DIM)
        .astype(jnp.bfloat16)
    )
    activated = jax.nn.gelu(hidden, approximate=True).astype(jnp.bfloat16)
    out_full, down_full = (
        lax.all_gather(w_out, "tm", axis=1, tiled=True),
        lax.all_gather(w_down, "tm", axis=1, tiled=True),
    )
    branches = jnp.dot(attended, out_full, preferred_element_type=jnp.float32)
    branches = branches + jnp.dot(activated, down_full, preferred_element_type=jnp.float32)
    mine = lax.psum_scatter(
        branches.astype(jnp.bfloat16), "tp", scatter_dimension=1, tiled=True
    ).astype(jnp.float32)
    features_here = mine.shape[1]
    first_feature = lax.axis_index("tp") * features_here
    normed_cols = lax.dynamic_slice_in_dim(normed_grid, first_feature, features_here, 2)
    padded = jnp.pad(normed_cols.astype(jnp.float32), ((4, 4), (0, 0), (0, 0)))
    extended = jnp.zeros((frames_here + 4, dancers_here, features_here), jnp.float32)
    for offset in range(KERNEL):
        extended = extended + conv_weight[offset] * padded[offset : offset + frames_here + 4]
    convolved = extended[2 : frames_here + 2]
    from_before = from_behind(extended[frames_here + 2 :], "tm", 1)
    from_after = from_behind(extended[0:2], "tm", -1)
    convolved = convolved.at[0:2].add(from_before)
    convolved = convolved.at[frames_here - 2 :].add(from_after)
    token_cols = lax.dynamic_slice_in_dim(tokens, first_feature, features_here, 2).astype(
        jnp.float32
    )
    result = token_cols + mine.reshape(frames_here, dancers_here, features_here) + convolved
    return result.astype(jnp.bfloat16)


def solution(mesh):
    placed = (
        P(("groups", "tm"), "ctx", None),
        P(),
        P(("groups", "tm"), "ctx", None),
        P("tm", "tp"),
        P("tm", "tp"),
        P("tm", "tp"),
        P("tp", "tm"),
        P("tm", "tp"),
        P("tp", "tm"),
        P(None, "tp"),
    )
    return jax.shard_map(
        on_device,
        mesh=mesh,
        in_specs=placed,
        out_specs=P(("groups", "tm"), "ctx", "tp"),
        check_vma=False,
    )
```

profile of v0, /device:TPU:0, one launch (start us, length us, event | category | flops | bytes accessed | tf_op | source)
XLA Modules:
  0.0 189.4 jit_solution(12623946930418223822)
XLA Ops:
  6.5 0.7 all-gather.7.cloned.1.call-update
  7.3 0.7 all-gather.9.cloned.1.call-update
  8.1 0.7 all-gather.11.cloned.1.call-update
  12.0 1.0 fusion.26
  13.0 19.9 %all-gather.7.cloned.1.call-done = bf16[1024,512]{1,0:T(8,128)(2,1)} async-done(((bf16[512,512]{1,0:T(8,128)(2,1)}), bf16[1024,512]{1,0:T(8,128)(2,1)}) %all-gather.7.cloned.1.call-update) | async-done | bytes 1048592 | tf_op jit(solution)/shard_map/all_gather | solution.py:30
  32.9 1.5 convolution_convert_fusion.2
  34.6 21.2 %all-gather.9.cloned.1.call-done = bf16[1024,512]{1,0:T(8,128)(2,1)} async-done(((bf16[512,512]{1,0:T(8,128)(2,1)}), bf16[1024,512]{1,0:T(8,128)(2,1)}) %all-gather.9.cloned.1.call-update) | async-done | bytes 1048592 | tf_op jit(solution)/shard_map/all_gather | solution.py:31
  55.8 1.5 convolution_convert_fusion.1
  57.4 15.5 %all_gather.26 = bf16[64,8,512]{2,0,1:T(8,128)(2,1)S(1)} all-gather(bf16[64,2,512]{2,0,1:T(8,128)(2,1)S(1)} %copy.35), channel_id=1, replica_groups=mesh['groups'=2,'ctx'=4,'tm'=2,'tp'=2] {'ctx'}, dimensions={1}, use_global_device_ids=true | all-gather | bytes 655360 | tf_op jit(solution)/shard_map/all_gather | solution.py:48
  73.7 5.0 %all-gather.11.cloned.1.call-done = bf16[1024,512]{1,0:T(8,128)(2,1)} async-done(((bf16[512,512]{1,0:T(8,128)(2,1)}), bf16[1024,512]{1,0:T(8,128)(2,1)}) %all-gather.11.cloned.1.call-update) | async-done | bytes 1048592 | tf_op jit(solution)/shard_map/all_gather | solution.py:32
  78.6 1.5 convolution_convert_fusion
  80.9 15.5 %all_gather.28 = bf16[64,8,512]{2,0,1:T(8,128)(2,1)S(1)} all-gather(bf16[64,2,512]{2,0,1:T(8,128)(2,1)S(1)} %copy.38), channel_id=1, replica_groups=mesh['groups'=2,'ctx'=4,'tm'=2,'tp'=2] {'ctx'}, dimensions={1}, use_global_device_ids=true | all-gather | bytes 655360 | tf_op jit(solution)/shard_map/all_gather | solution.py:49
  96.6 1.5 reshape.132
  99.4 0.9 fusion.5
  100.2 12.9 %all-gather.17.cloned.1.call-done = bf16[1024,1024]{1,0:T(8,128)(2,1)} async-done(((bf16[1024,512]{1,0:T(8,128)(2,1)}), bf16[1024,1024]{1,0:T(8,128)(2,1)}) %all-gather.17.cloned.1.call-update) | async-done | bytes 2097168 | tf_op jit(solution)/shard_map/all_gather | solution.py:76
  113.2 34.5 %all-gather.15.cloned.1.call-done = bf16[1024,1024]{1,0:T(8,128)(2,1)} async-done(((bf16[512,1024]{1,0:T(8,128)(2,1)}), bf16[1024,1024]{1,0:T(8,128)(2,1)}) %all-gather.15.cloned.1.call-update) | async-done | bytes 2097168 | tf_op jit(solution)/shard_map/all_gather | solution.py:33
  147.7 3.1 %fusion.30 = f32[128,1024]{1,0:T(8,128)S(1)} fusion(bf16[1024,1024]{1,0:T(8,128)(2,1)} %all-gather.17.cloned.1.call-done, bf16[128,1024]{1,0:T(8,128)(2,1)S(1)} %reshape.127, bf16[1024,1024]{1,0:T(8,128)(2,1)} %all-gather.15.cloned.1.call-done), kind=kOutput, calls=%fused_computation.45 | convolution fusion | flops 538050560 | bytes 4980736 | tf_op jit(solution)/shard_map/dot_general | solution.py:79
  150.8 19.6 %all-gather.13.cloned.1.call-done = bf16[512,1024]{1,0:T(8,128)(2,1)} async-done(((bf16[512,512]{1,0:T(8,128)(2,1)}), bf16[512,1024]{1,0:T(8,128)(2,1)}) %all-gather.13.cloned.1.call-update) | async-done | bytes 1048592 | tf_op jit(solution)/shard_map/all_gather | solution.py:75
  170.4 2.3 %fusion.3 = bf16[128,1024]{1,0:T(8,128)(2,1)} fusion(f32[128,1024]{1,0:T(8,128)S(1)} %fusion.30, bf16[128,512]{0,1:T(8,128)(2,1)S(1)} %bitcast.34, bf16[512,1024]{1,0:T(8,128)(2,1)} %all-gather.13.cloned.1.call-done), kind=kOutput, calls=%fused_computation.6 | convolution fusion | flops 134479872 | bytes 1966080 | tf_op jit(solution)/shard_map/dot_general | solution.py:78
  172.7 2.3 %collective-permute-start = (f32[2,2,512]{2,1,0:T(2,128)S(1)}, f32[2,2,512]{2,1,0:T(2,128)S(1)}, u32[]{:S(2)}, u32[]{:S(2)}) collective-permute-start(f32[2,2,512]{2,1,0:T(2,128)S(1)} %get-tuple-element.30), channel_id=1, source_target_pairs={{0,2},{1,3},{4,6},{5,7},{8,10},{9,11},{12,14},{13,15},{16,18},{17,... | collective-permute-start | bytes 24584 | tf_op jit(solution)/shard_map/ppermute | solution.py:13
  175.0 1.3 collective-permute-start.1
  176.3 4.2 %collective-permute-done.1 = f32[2,2,512]{2,1,0:T(2,128)S(1)} collective-permute-done((f32[2,2,512]{2,1,0:T(2,128)S(1)}, f32[2,2,512]{2,1,0:T(2,128)S(1)}, u32[]{:S(2)}, u32[]{:S(2)}) %collective-permute-start.1) | collective-permute-done | bytes 8224 | tf_op jit(solution)/shard_map/ppermute | solution.py:13
  180.6 1.1 reshape.136
  181.7 0.8 add_convert_fusion
  (55 shorter events, 6.5 us)
Async XLA Ops:
  6.5 4.0 %copy-start = (bf16[64,2,1024]{2,1,0:T(2,128)(2,1)S(1)}, bf16[64,2,1024]{2,1,0:T(2,128)(2,1)}, u32[]{:S(2)}) copy-start(bf16[64,2,1024]{2,1,0:T(2,128)(2,1)} %param.14) | copy-start | bytes 786436
  6.5 26.4 %all-gather.7.cloned.1.call-start = ((), (), s32[]{:S(2)}) async-start(), calls=%async_computation.1 | async-start | bytes 1572864 | tf_op jit(solution)/shard_map/all_gather | solution.py:30
  7.3 3.7 %copy-start.5 = (f32[1024]{0:T(1024)S(1)}, f32[1024]{0:T(1024)}, u32[]{:S(2)}) copy-start(f32[1024]{0:T(1024)} %param.15) | copy-start | bytes 12292
  7.3 48.5 %all-gather.9.cloned.1.call-start = ((), (), s32[]{:S(2)}) async-start(), calls=%async_computation.2 | async-start | bytes 1572864 | tf_op jit(solution)/shard_map/all_gather | solution.py:31
  8.0 70.6 %all-gather.11.cloned.1.call-start = ((), (), s32[]{:S(2)}) async-start(), calls=%async_computation.3 | async-start | bytes 1572864 | tf_op jit(solution)/shard_map/all_gather | solution.py:32
  8.8 104.4 %all-gather.17.cloned.1.call-start = ((), (), s32[]{:S(2)}) async-start(), calls=%async_computation.6 | async-start | bytes 3145728 | tf_op jit(solution)/shard_map/all_gather | solution.py:76
  9.3 2.3 %copy-start.4 = (f32[5,512]{1,0:T(8,128)S(1)}, f32[5,512]{1,0:T(8,128)}, u32[]{:S(2)}) copy-start(f32[5,512]{1,0:T(8,128)} %param.23) | copy-start | bytes 30724
  9.3 2.3 %copy-start.6 = (s32[1,1,4]{2,1,0:T(1,128)S(1)}, s32[1,1,4]{2,1,0:T(1,128)}, u32[]{:S(2)}) copy-start(s32[1,1,4]{2,1,0:T(1,128)} %param.16) | copy-start | bytes 52
  9.3 138.3 %all-gather.15.cloned.1.call-start = ((), (), s32[]{:S(2)}) async-start(), calls=%async_computation.5 | async-start | bytes 3145728 | tf_op jit(solution)/shard_map/all_gather | solution.py:33
  9.9 160.5 %all-gather.13.cloned.1.call-start = ((), (), s32[]{:S(2)}) async-start(), calls=%async_computation.4 | async-start | bytes 1572864 | tf_op jit(solution)/shard_map/all_gather | solution.py:75
  10.5 170.1 %reduce-scatter.2.cloned.1.call-start = ((), (), s32[]{:S(2)}) async-start(), calls=%async_computation.7 | async-start | bytes 393216 | tf_op jit(solution)/shard_map/reduce_scatter | solution.py:80
  98.1 1.2 copy-start.3
  150.7 21.9 %copy-start.2 = (f32[68,2,512]{2,1,0:T(2,128)S(1)}, f32[68,2,512]{2,1,0:T(2,128)}, u32[]{:S(2)}) copy-start(f32[68,2,512]{2,1,0:T(2,128)} %fusion.26) | copy-start | bytes 835588
  150.8 25.5 %slice-start = ((f32[68,2,512]{2,1,0:T(2,128)}), f32[64,2,512]{2,1,0:T(2,128)S(1)}, s32[]{:S(2)}) async-start(f32[68,2,512]{2,1,0:T(2,128)} %fusion.26), calls=%async_computation.8 | async-start | bytes 524288 | tf_op jit(solution)/shard_map/slice | solution.py:90
  150.8 30.9 %copy-start.1 = (bf16[64,2,1024]{2,1,0:T(2,128)(2,1)S(1)}, bf16[64,2,1024]{2,1,0:T(2,128)(2,1)}, u32[]{:S(2)}) copy-start(bf16[64,2,1024]{2,1,0:T(2,128)(2,1)} %param.14) | copy-start | bytes 786436
  172.7 3.6 %collective-permute-start = (f32[2,2,512]{2,1,0:T(2,128)S(1)}, f32[2,2,512]{2,1,0:T(2,128)S(1)}, u32[]{:S(2)}, u32[]{:S(2)}) collective-permute-start(f32[2,2,512]{2,1,0:T(2,128)S(1)} %get-tuple-element.30), channel_id=1, source_target_pairs={{0,2},{1,3},{4,6},{5,7},{8,10},{9,11},{12,14},{13,15},{16,18},{17,... | collective-permute-start | bytes 24584 | tf_op jit(solution)/shard_map/ppermute | solution.py:13
  175.0 5.5 %collective-permute-start.1 = (f32[2,2,512]{2,1,0:T(2,128)S(1)}, f32[2,2,512]{2,1,0:T(2,128)S(1)}, u32[]{:S(2)}, u32[]{:S(2)}) collective-permute-start(f32[2,2,512]{2,1,0:T(2,128)S(1)} %get-tuple-element.29), channel_id=1, source_target_pairs={{2,0},{3,1},{6,4},{7,5},{10,8},{11,9},{14,12},{15,13},{18,16},{19,... | collective-permute-start | bytes 24584 | tf_op jit(solution)/shard_map/ppermute | solution.py:13
Sparse Core Ops, SparseCore 0:
  8.9 23.9 all-gather.6
  34.5 21.2 all-gather.8
  57.3 21.2 all-gather.10
  80.0 33.0 all-gather.16
  114.5 33.0 all-gather.14
  149.1 21.2 all-gather.12
  172.8 7.7 reduce-scatter.1
where the time goes:
time: 190 us; the launch traced here: 189 us
  waiting for transfers between devices  121 us (64%)
  blocking collectives  30.9 us (16%)
  between operations  13.8 us (7%)
  matrix products  11.6 us (6%)
  local copies, waits for them, and re-layouts  4.94 us (3%)
  starting transfers between devices  3.77 us (2%)
  other arithmetic  3.36 us (2%)
    all_gather x1, waiting for transfers between devices, on_device(): lax.all_gather(w_up, 'tm', axis=0, tiled=True)  34.5 us
    all_gather x1, waiting for transfers between devices, on_device(): lax.all_gather(w_key, 'tm', axis=0, tiled=True)  21.2 us
    all_gather x1, waiting for transfers between devices, on_device(): lax.all_gather(w_query, 'tm', axis=0, tiled=True)  19.9 us
    all_gather x1, waiting for transfers between devices, on_device(): lax.all_gather(w_out, 'tm', axis=1, tiled=True)  19.6 us
    all_gather x1, blocking collectives, on_device(): key_piece = lax.all_gather(key_grid, 'ctx', axis=1, tiled=True)  15.5 us
    all_gather x1, blocking collectives, on_device(): value_piece = lax.all_gather(value_grid, 'ctx', axis=1, tiled=True)  15.5 us
    all_gather x1, waiting for transfers between devices, on_device(): lax.all_gather(w_down, 'tm', axis=1, tiled=True)  12.9 us
    all_gather x1, waiting for transfers between devices, on_device(): lax.all_gather(w_value, 'tm', axis=0, tiled=True)  4.95 us
  transfers between devices with their start and end apart: 9, of which 8 were waited for; matrix products, arithmetic and copies ran while one was open for 8% of the time, Pallas kernels for 0%

commit v1 on v0

--- a/solution.py
+++ b/solution.py
@@ -27,7 +27,9 @@
     normed_grid = rms_norm(tokens, norm_gain)
     normed = normed_grid.reshape(rows_here, width)
     pieces = (
-        lax.all_gather(w_query, "tm", axis=0, tiled=True),
+        jnp.concatenate(
+            lax.all_to_all(jnp.stack([w_query] * lax.axis_size("tm")), "tm", 0, 0), axis=0
+        ),
         lax.all_gather(w_key, "tm", axis=0, tiled=True),
         lax.all_gather(w_value, "tm", axis=0, tiled=True),
         lax.all_gather(w_up, "tm", axis=0, tiled=True),

time: 190 us -> 176 us (0.926)
  waiting for transfers between devices: 121 us -> 102 us
  starting transfers between devices: 3.77 us -> 8.06 us
    all_to_all x0 -> x1, waiting for transfers between devices: none -> 20 us  [on_device(): lax.all_to_all(jnp.stack([w_query] * lax.axis_size('tm')), 'tm', 0, 0)]
    all_gather x1 -> x0, waiting for transfers between devices: 19.9 us -> none  [on_device(): lax.all_gather(w_query, 'tm', axis=0, tiled=True)]
    all_gather x1, waiting for transfers between devices: 21.2 us -> 2.41 us  [on_device(): lax.all_gather(w_key, 'tm', axis=0, tiled=True)]
    all_to_all x0 -> x1, starting transfers between devices: none -> 4.37 us  [on_device(): lax.all_to_all(jnp.stack([w_query] * lax.axis_size('tm')), 'tm', 0, 0)]
  transfers between devices with their start and end apart: 9 -> 9, of which waited for: 8 -> 8; matrix products, arithmetic and copies ran while one was open for 8% -> 9% of each run, Pallas kernels for 0% -> 0%
where the time goes in v1:
time: 176 us; the launch traced here: 175 us
  waiting for transfers between devices  102 us (58%)
  blocking collectives  31.7 us (18%)
  between operations  13.7 us (8%)
  matrix products  10.4 us (6%)
  starting transfers between devices  8.06 us (5%)
  local copies, waits for them, and re-layouts  4.94 us (3%)
  other arithmetic  4.51 us (3%)
    all_gather x1, waiting for transfers between devices, on_device(): lax.all_gather(w_up, 'tm', axis=0, tiled=True)  34.5 us
    all_to_all x1, waiting for transfers between devices, on_device(): lax.all_to_all(jnp.stack([w_query] * lax.axis_size('tm')), 'tm', 0, 0)  20 us
    all_gather x1, waiting for transfers between devices, on_device(): lax.all_gather(w_out, 'tm', axis=1, tiled=True)  19.6 us
    all_gather x1, blocking collectives, on_device(): key_piece = lax.all_gather(key_grid, 'ctx', axis=1, tiled=True)  16.2 us
    all_gather x1, blocking collectives, on_device(): value_piece = lax.all_gather(value_grid, 'ctx', axis=1, tiled=True)  15.5 us
    all_gather x1, waiting for transfers between devices, on_device(): lax.all_gather(w_down, 'tm', axis=1, tiled=True)  13.1 us
    all_gather x1, waiting for transfers between devices, on_device(): lax.all_gather(w_value, 'tm', axis=0, tiled=True)  4.73 us
    all_to_all x1, starting transfers between devices, on_device(): lax.all_to_all(jnp.stack([w_query] * lax.axis_size('tm')), 'tm', 0, 0)  4.37 us
  transfers between devices with their start and end apart: 9, of which 8 were waited for; matrix products, arithmetic and copies ran while one was open for 9% of the time, Pallas kernels for 0%

profile of v1, /device:TPU:0, one launch (start us, length us, event | category | flops | bytes accessed | tf_op | source)
XLA Modules:
  0.0 175.1 jit_solution(6878374878553459795)
XLA Ops:
  6.5 0.7 all-gather.6.cloned.1.call-update
  7.3 0.7 all-gather.8.cloned.1.call-update
  9.4 1.1 pad_maximum_fusion
  10.5 4.4 %all-to-all-start = ((bf16[2,512,512]{2,1,0:T(8,128)(2,1)}), bf16[2,512,512]{2,1,0:T(8,128)(2,1)S(1)}, u32[]{:S(2)}, u32[]{:S(2)}) async-start(bf16[2,512,512]{2,1,0:T(8,128)(2,1)} %pad_maximum_fusion), calls=%async_computation | async-start | bytes 2097152 | tf_op jit(solution)/shard_map/all_to_all | solution.py:31
  16.9 1.0 fusion.26
  18.0 20.0 %all-to-all-done = bf16[2,512,512]{2,1,0:T(8,128)(2,1)S(1)} async-done(((bf16[2,512,512]{2,1,0:T(8,128)(2,1)}), bf16[2,512,512]{2,1,0:T(8,128)(2,1)S(1)}, u32[]{:S(2)}, u32[]{:S(2)}) %all-to-all-start) | async-done | bytes 1048608 | tf_op jit(solution)/shard_map/all_to_all | solution.py:31
  38.4 2.4 %all-gather.6.cloned.1.call-done = bf16[1024,512]{1,0:T(8,128)(2,1)} async-done(((bf16[512,512]{1,0:T(8,128)(2,1)}), bf16[1024,512]{1,0:T(8,128)(2,1)}) %all-gather.6.cloned.1.call-update) | async-done | bytes 1048592 | tf_op jit(solution)/shard_map/all_gather | solution.py:33
  40.8 1.5 convolution_convert_fusion.1
  42.4 16.2 %all_gather.22 = bf16[64,8,512]{2,0,1:T(8,128)(2,1)S(1)} all-gather(bf16[64,2,512]{2,0,1:T(8,128)(2,1)S(1)} %copy.35), channel_id=1, replica_groups=mesh['groups'=2,'ctx'=4,'tm'=2,'tp'=2] {'ctx'}, dimensions={1}, use_global_device_ids=true | all-gather | bytes 655360 | tf_op jit(solution)/shard_map/all_gather | solution.py:50
  59.5 4.7 %all-gather.8.cloned.1.call-done = bf16[1024,512]{1,0:T(8,128)(2,1)} async-done(((bf16[512,512]{1,0:T(8,128)(2,1)}), bf16[1024,512]{1,0:T(8,128)(2,1)}) %all-gather.8.cloned.1.call-update) | async-done | bytes 1048592 | tf_op jit(solution)/shard_map/all_gather | solution.py:34
  64.2 1.5 convolution_convert_fusion
  66.4 15.5 %all_gather.24 = bf16[64,8,512]{2,0,1:T(8,128)(2,1)S(1)} all-gather(bf16[64,2,512]{2,0,1:T(8,128)(2,1)S(1)} %copy.38), channel_id=1, replica_groups=mesh['groups'=2,'ctx'=4,'tm'=2,'tp'=2] {'ctx'}, dimensions={1}, use_global_device_ids=true | all-gather | bytes 655360 | tf_op jit(solution)/shard_map/all_gather | solution.py:51
  82.2 1.5 reshape.136
  84.9 0.9 fusion.5
  85.8 13.1 %all-gather.14.cloned.1.call-done = bf16[1024,1024]{1,0:T(8,128)(2,1)} async-done(((bf16[1024,512]{1,0:T(8,128)(2,1)}), bf16[1024,1024]{1,0:T(8,128)(2,1)}) %all-gather.14.cloned.1.call-update) | async-done | bytes 2097168 | tf_op jit(solution)/shard_map/all_gather | solution.py:78
  98.9 34.5 %all-gather.12.cloned.1.call-done = bf16[1024,1024]{1,0:T(8,128)(2,1)} async-done(((bf16[512,1024]{1,0:T(8,128)(2,1)}), bf16[1024,1024]{1,0:T(8,128)(2,1)}) %all-gather.12.cloned.1.call-update) | async-done | bytes 2097168 | tf_op jit(solution)/shard_map/all_gather | solution.py:35
  133.4 3.1 %fusion.30 = f32[128,1024]{1,0:T(8,128)S(1)} fusion(bf16[1024,1024]{1,0:T(8,128)(2,1)} %all-gather.14.cloned.1.call-done, bf16[128,1024]{1,0:T(8,128)(2,1)S(1)} %reshape.130, bf16[1024,1024]{1,0:T(8,128)(2,1)} %all-gather.12.cloned.1.call-done), kind=kOutput, calls=%fused_computation.46 | convolution fusion | flops 538050560 | bytes 4980736 | tf_op jit(solution)/shard_map/dot_general | solution.py:81
  136.5 19.6 %all-gather.10.cloned.1.call-done = bf16[512,1024]{1,0:T(8,128)(2,1)} async-done(((bf16[512,512]{1,0:T(8,128)(2,1)}), bf16[512,1024]{1,0:T(8,128)(2,1)}) %all-gather.10.cloned.1.call-update) | async-done | bytes 1048592 | tf_op jit(solution)/shard_map/all_gather | solution.py:77
  156.1 2.3 %fusion.3 = bf16[128,1024]{1,0:T(8,128)(2,1)} fusion(f32[128,1024]{1,0:T(8,128)S(1)} %fusion.30, bf16[128,512]{0,1:T(8,128)(2,1)S(1)} %bitcast.38, bf16[512,1024]{1,0:T(8,128)(2,1)} %all-gather.10.cloned.1.call-done), kind=kOutput, calls=%fused_computation.6 | convolution fusion | flops 134479872 | bytes 1966080 | tf_op jit(solution)/shard_map/dot_general | solution.py:80
  158.4 2.3 %collective-permute-start = (f32[2,2,512]{2,1,0:T(2,128)S(1)}, f32[2,2,512]{2,1,0:T(2,128)S(1)}, u32[]{:S(2)}, u32[]{:S(2)}) collective-permute-start(f32[2,2,512]{2,1,0:T(2,128)S(1)} %get-tuple-element.30), channel_id=1, source_target_pairs={{0,2},{1,3},{4,6},{5,7},{8,10},{9,11},{12,14},{13,15},{16,18},{17,... | collective-permute-start | bytes 24584 | tf_op jit(solution)/shard_map/ppermute | solution.py:13
  160.7 1.3 collective-permute-start.1
  162.0 4.2 %collective-permute-done.1 = f32[2,2,512]{2,1,0:T(2,128)S(1)} collective-permute-done((f32[2,2,512]{2,1,0:T(2,128)S(1)}, f32[2,2,512]{2,1,0:T(2,128)S(1)}, u32[]{:S(2)}, u32[]{:S(2)}) %collective-permute-start.1) | collective-permute-done | bytes 8224 | tf_op jit(solution)/shard_map/ppermute | solution.py:13
  166.3 1.1 reshape.140
  167.4 0.8 add_convert_fusion
  (57 shorter events, 6.9 us)
Async XLA Ops:
  6.5 2.8 %copy-start.4 = (bf16[512,512]{1,0:T(8,128)(2,1)S(1)}, bf16[512,512]{1,0:T(8,128)(2,1)}, u32[]{:S(2)}) copy-start(bf16[512,512]{1,0:T(8,128)(2,1)} %param.17) | copy-start | bytes 1572868
  6.5 34.2 %all-gather.6.cloned.1.call-start = ((), (), s32[]{:S(2)}) async-start(), calls=%async_computation.2 | async-start | bytes 1572864 | tf_op jit(solution)/shard_map/all_gather | solution.py:33
  7.3 57.0 %all-gather.8.cloned.1.call-start = ((), (), s32[]{:S(2)}) async-start(), calls=%async_computation.3 | async-start | bytes 1572864 | tf_op jit(solution)/shard_map/all_gather | solution.py:34
  8.0 90.9 %all-gather.14.cloned.1.call-start = ((), (), s32[]{:S(2)}) async-start(), calls=%async_computation.6 | async-start | bytes 3145728 | tf_op jit(solution)/shard_map/all_gather | solution.py:78
  8.7 124.7 %all-gather.12.cloned.1.call-start = ((), (), s32[]{:S(2)}) async-start(), calls=%async_computation.5 | async-start | bytes 3145728 | tf_op jit(solution)/shard_map/all_gather | solution.py:35
  9.3 6.2 %copy-start = (bf16[64,2,1024]{2,1,0:T(2,128)(2,1)S(1)}, bf16[64,2,1024]{2,1,0:T(2,128)(2,1)}, u32[]{:S(2)}) copy-start(bf16[64,2,1024]{2,1,0:T(2,128)(2,1)} %param.14) | copy-start | bytes 786436
  9.3 6.5 %copy-start.6 = (f32[1024]{0:T(1024)S(1)}, f32[1024]{0:T(1024)}, u32[]{:S(2)}) copy-start(f32[1024]{0:T(1024)} %param.15) | copy-start | bytes 12292
  10.5 6.0 %copy-start.7 = (s32[1,1,4]{2,1,0:T(1,128)S(1)}, s32[1,1,4]{2,1,0:T(1,128)}, u32[]{:S(2)}) copy-start(s32[1,1,4]{2,1,0:T(1,128)} %param.16) | copy-start | bytes 52
  10.5 6.4 %copy-start.5 = (f32[5,512]{1,0:T(8,128)S(1)}, f32[5,512]{1,0:T(8,128)}, u32[]{:S(2)}) copy-start(f32[5,512]{1,0:T(8,128)} %param.23) | copy-start | bytes 30724
  10.5 27.4 %all-to-all-start = ((bf16[2,512,512]{2,1,0:T(8,128)(2,1)}), bf16[2,512,512]{2,1,0:T(8,128)(2,1)S(1)}, u32[]{:S(2)}, u32[]{:S(2)}) async-start(bf16[2,512,512]{2,1,0:T(8,128)(2,1)} %pad_maximum_fusion), calls=%async_computation | async-start | bytes 2097152 | tf_op jit(solution)/shard_map/all_to_all | solution.py:31
  14.9 141.2 %all-gather.10.cloned.1.call-start = ((), (), s32[]{:S(2)}) async-start(), calls=%async_computation.4 | async-start | bytes 1572864 | tf_op jit(solution)/shard_map/all_gather | solution.py:77
  15.4 150.9 %reduce-scatter.2.cloned.1.call-start = ((), (), s32[]{:S(2)}) async-start(), calls=%async_computation.7 | async-start | bytes 393216 | tf_op jit(solution)/shard_map/reduce_scatter | solution.py:82
  83.7 1.2 copy-start.3
  136.5 21.9 %copy-start.2 = (f32[68,2,512]{2,1,0:T(2,128)S(1)}, f32[68,2,512]{2,1,0:T(2,128)}, u32[]{:S(2)}) copy-start(f32[68,2,512]{2,1,0:T(2,128)} %fusion.26) | copy-start | bytes 835588
  136.5 25.5 %slice-start = ((f32[68,2,512]{2,1,0:T(2,128)}), f32[64,2,512]{2,1,0:T(2,128)S(1)}, s32[]{:S(2)}) async-start(f32[68,2,512]{2,1,0:T(2,128)} %fusion.26), calls=%async_computation.8 | async-start | bytes 524288 | tf_op jit(solution)/shard_map/slice | solution.py:92
  136.5 30.9 %copy-start.1 = (bf16[64,2,1024]{2,1,0:T(2,128)(2,1)S(1)}, bf16[64,2,1024]{2,1,0:T(2,128)(2,1)}, u32[]{:S(2)}) copy-start(bf16[64,2,1024]{2,1,0:T(2,128)(2,1)} %param.14) | copy-start | bytes 786436
  158.4 3.6 %collective-permute-start = (f32[2,2,512]{2,1,0:T(2,128)S(1)}, f32[2,2,512]{2,1,0:T(2,128)S(1)}, u32[]{:S(2)}, u32[]{:S(2)}) collective-permute-start(f32[2,2,512]{2,1,0:T(2,128)S(1)} %get-tuple-element.30), channel_id=1, source_target_pairs={{0,2},{1,3},{4,6},{5,7},{8,10},{9,11},{12,14},{13,15},{16,18},{17,... | collective-permute-start | bytes 24584 | tf_op jit(solution)/shard_map/ppermute | solution.py:13
  160.7 5.5 %collective-permute-start.1 = (f32[2,2,512]{2,1,0:T(2,128)S(1)}, f32[2,2,512]{2,1,0:T(2,128)S(1)}, u32[]{:S(2)}, u32[]{:S(2)}) collective-permute-start(f32[2,2,512]{2,1,0:T(2,128)S(1)} %get-tuple-element.29), channel_id=1, source_target_pairs={{2,0},{3,1},{6,4},{7,5},{10,8},{11,9},{14,12},{15,13},{18,16},{19,... | collective-permute-start | bytes 24584 | tf_op jit(solution)/shard_map/ppermute | solution.py:13
Sparse Core Ops, SparseCore 0:
  8.9 31.8 all-gather.5
  42.3 21.8 all-gather.7
  65.8 33.0 all-gather.13
  100.3 33.0 all-gather.11
  134.8 21.2 all-gather.9
  158.5 7.7 reduce-scatter.1
